TPU v7x, 32 devices: a whole 2x2x4 slice. The times are simulated.
32 devices in a mesh: grp: 2 (over x), seq: 16 (over z, y, core).
Axes of the slice: x: 2, y: 2, z: 4, core: 2. Of those that a mesh axis runs over, the one named last changes fastest.
Arguments:
- events: bfloat16 [24576, 1024], P(('grp', 'seq')), parts along dimension 0, may hold values from -6 to 6
- w_query: bfloat16 [1024, 1024], replicated, may hold values from -0.1875 to 0.1875
- w_key: bfloat16 [1024, 1024], replicated, may hold values from -0.1875 to 0.1875
- w_value: bfloat16 [1024, 1024], replicated, may hold values from -0.1875 to 0.1875
- w_output: bfloat16 [1024, 1024], replicated, may hold values from -0.1875 to 0.1875
- expert_in: bfloat16 [1024, 16384], P(None, 'seq'), may hold values from -0.1875 to 0.1875
- expert_out: bfloat16 [16384, 256], P('seq'), may hold values from -0.1875 to 0.1875
- gate_weight: bfloat16 [1024, 32], replicated, may hold values from -0.1875 to 0.1875
- label_rows: int32 [1024], P(('grp', 'seq')), parts along dimension 0, may hold values from 0 to 767
- label_experts: int32 [1024, 2], P(('grp', 'seq')), parts along dimension 0, may hold values from 0 to 15, all different within a row; in each aligned block of 32 rows (0 to 31, 32 to 63, ...) at most 8 rows name the same one
- label_tasks: int32 [1024], P(('grp', 'seq')), parts along dimension 0, may hold values from 0 to 1
Outputs:
- hidden: bfloat16 [24576, 1024], P(('grp', 'seq')), parts along dimension 0
- scores: float32 [1024, 256], P(('grp', 'seq')), parts along dimension 0
There are 2 independent parts, one for each index of `grp`. A program takes and returns all parts, laid end to end along the dimension named above; an argument that names none is the same for every part. Nothing has to cross between parts.
Inputs may be any that keep to these rules, and one draw needn't show every extreme that they name: `label_experts`: each row names two different experts; within the 32 rows of one device (aligned blocks) no expert is named by more than 8 rows, and in every draw some expert is named by exactly 8 rows of some device.
All inputs are finite; a program needn't handle non-finite values.
Results may differ from a plain program's by a relative error of at most 0.012.
Values may be sent and summed in bfloat16 or wider, within the bound.
A program may use at most 128 MiB of HBM per device.

v0:
```python
import jax
import jax.numpy as jnp
from jax import lax
from jax.sharding import PartitionSpec as P

HEADS = 8
EXPERTS = 16
CAP = 8


def carried_in(shard, axis, combine, identity):
    length, position = (lax.axis_size(axis), lax.axis_index(axis))
    everything = lax.all_gather(shard, axis)
    start = jnp.broadcast_to(jnp.asarray(identity, shard.dtype), shard.shape)

    def step(k, before):
        reached = k < position
        new = combine(before, everything[k])
        return jnp.where(reached, new, before)

    return lax.fori_loop(0, length, step, start)


def slot_places(route):
    flat = route.reshape(-1)
    onehot = (flat[:, None] == jnp.arange(EXPERTS, dtype=jnp.int32)[None, :]).astype(jnp.int32)
    before = jnp.cumsum(onehot, axis=0) - onehot
    slot_index = jnp.sum(before * onehot, axis=1)
    return (flat * CAP + slot_index).reshape(route.shape)


def expert_rows(arrived, weight_in, weight_out):
    count_src = arrived.shape[0]
    count_slot = arrived.shape[1]
    flat = arrived.reshape(count_src * count_slot, arrived.shape[2])
    inner = jax.nn.relu(jnp.dot(flat, weight_in, preferred_element_type=jnp.float32)).astype(
        jnp.bfloat16
    )
    partial_sum = jnp.dot(inner, weight_out, preferred_element_type=jnp.float32)
    return partial_sum.reshape(count_src, count_slot, partial_sum.shape[1])


def add_states(earlier, later):
    return earlier + later


def shards(
    events,
    w_query,
    w_key,
    w_value,
    w_output,
    expert_in,
    expert_out,
    gate_weight,
    label_rows,
    label_experts,
    label_tasks,
):
    tok_rows = events.shape[0]
    width = events.shape[1]
    head_dim = width // HEADS
    query = (
        jnp.dot(events, w_query, preferred_element_type=jnp.float32)
        .astype(jnp.bfloat16)
        .reshape(tok_rows, HEADS, head_dim)
    )
    keys = (
        jnp.dot(events, w_key, preferred_element_type=jnp.float32)
        .astype(jnp.bfloat16)
        .reshape(tok_rows, HEADS, head_dim)
    )
    values = (
        jnp.dot(events, w_value, preferred_element_type=jnp.float32)
        .astype(jnp.bfloat16)
        .reshape(tok_rows, HEADS, head_dim)
    )
    local_state = jnp.einsum("shd,she->hde", keys, values, preferred_element_type=jnp.float32)
    identity = jnp.zeros_like(local_state)
    prefix = carried_in(local_state, "seq", add_states, identity).astype(jnp.bfloat16)
    local_index = jnp.arange(tok_rows, dtype=jnp.int32)
    causal = local_index[None, :] <= local_index[:, None]
    weight = jnp.einsum("thd,shd->hts", query, keys, preferred_element_type=jnp.float32)
    weight = jnp.where(causal[None], weight, 0.0).astype(jnp.bfloat16)
    within = jnp.einsum("hts,shd->thd", weight, values, preferred_element_type=jnp.float32)
    earlier = jnp.einsum("thd,hde->the", query, prefix, preferred_element_type=jnp.float32)
    places_now = lax.axis_index("seq") * tok_rows + local_index
    factor = lax.rsqrt((places_now + 1).astype(jnp.float32) * head_dim)
    attended = (
        ((within + earlier) * factor[:, None, None]).astype(jnp.bfloat16).reshape(tok_rows, width)
    )
    hidden = (
        events.astype(jnp.float32) + jnp.dot(attended, w_output, preferred_element_type=jnp.float32)
    ).astype(jnp.bfloat16)
    picked = jnp.take(hidden, label_rows, axis=0)
    places = slot_places(label_experts)
    copies = lax.axis_size("seq") // EXPERTS
    targets = jnp.arange(EXPERTS * CAP, dtype=jnp.int32)
    selector = jnp.any(targets[:, None, None] == places[None, :, :], axis=2).astype(jnp.bfloat16)
    buffer = jnp.dot(selector, picked, preferred_element_type=jnp.float32).astype(jnp.bfloat16)
    outgoing = jnp.repeat(buffer.reshape(EXPERTS, CAP, width), copies, axis=0)
    partials = expert_rows(
        lax.all_to_all(outgoing, "seq", split_axis=0, concat_axis=0, tiled=True),
        expert_in,
        expert_out,
    )
    back = lax.all_to_all(
        partials.astype(jnp.bfloat16), "seq", split_axis=0, concat_axis=0, tiled=True
    ).astype(partials.dtype)
    out_width = back.shape[2]
    totals = (
        back.reshape(EXPERTS, copies, CAP, out_width).sum(axis=1).reshape(EXPERTS * CAP, out_width)
    )
    chosen = jnp.take(totals, places.reshape(-1), axis=0).reshape(places.shape[0], 2, out_width)
    logits = jnp.dot(picked, gate_weight, preferred_element_type=jnp.float32)
    columns = label_tasks[:, None] * EXPERTS + label_experts
    gates = jax.nn.sigmoid(jnp.take_along_axis(logits, columns, axis=1))
    scores = jnp.sum(gates[:, :, None] * chosen, axis=1)
    return (hidden, scores)


def solution(mesh):
    placed = (
        P(("grp", "seq"), None),
        P(),
        P(),
        P(),
        P(),
        P(None, "seq"),
        P("seq", None),
        P(),
        P(("grp", "seq")),
        P(("grp", "seq"), None),
        P(("grp", "seq")),
    )
    return jax.shard_map(
        shards,
        mesh=mesh,
        in_specs=placed,
        out_specs=(P(("grp", "seq"), None), P(("grp", "seq"), None)),
        check_vma=False,
    )
```

profile of v0, /device:TPU:0, one launch (start us, length us, event | category | flops | bytes accessed | tf_op | source)
XLA Modules:
  0.0 164.3 jit_solution(9241055167782557303)
XLA Ops:
  7.2 1.5 copy-done
  8.8 4.3 %convolution_convert_fusion = bf16[768,1024]{1,0:T(8,128)(2,1)} fusion(bf16[768,1024]{1,0:T(8,128)(2,1)} %param.13, bf16[1024,1024]{1,0:T(8,128)(2,1)S(1)} %copy-done), kind=kOutput, calls=%fused_computation.12 | convolution fusion | flops 1611399168 | bytes 5242880 | tf_op jit(solution)/shard_map/dot_general | solution.py:69
  13.1 2.6 %copy.73 = bf16[768,1024]{0,1:T(8,128)(2,1)} copy(bf16[768,1024]{1,0:T(8,128)(2,1)} %convolution_convert_fusion) | data formatting | bytes 3145728 | tf_op jit(solution)/shard_map/reshape | solution.py:71
  15.7 4.0 %fusion.11 = bf16[96,8,8,128]{3,2,1,0:T(8,128)(2,1)S(1)} fusion(bf16[768,1024]{1,0:T(8,128)(2,1)} %param.13, bf16[1024,1024]{1,0:T(8,128)(2,1)} %param.16), kind=kOutput, calls=%fused_computation.20 | convolution fusion | flops 1611399168 | bytes 5242880 | tf_op jit(solution)/shard_map/dot_general | solution.py:74
  19.7 1.1 copy-done.9
  20.9 1.4 fusion.9
  22.4 0.1 reshape.130
  22.6 0.1 reduce_window_sum.11
  22.7 0.2 select_reduce_fusion
  22.9 0.1 reduce_sum.27
  23.2 0.1 mul.72
  23.4 0.1 reshape.152
  23.5 0.1 copy.70
  23.7 0.2 iota_compare_fusion
  23.9 5.0 %fusion.12 = bf16[96,8,8,128]{3,2,1,0:T(8,128)(2,1)} fusion(bf16[768,1024]{1,0:T(8,128)(2,1)} %param.13, bf16[1024,1024]{1,0:T(8,128)(2,1)} %param.14), kind=kOutput, calls=%fused_computation.21 | convolution fusion | flops 1611399168 | bytes 5242880 | tf_op jit(solution)/shard_map/dot_general | solution.py:64
  28.9 9.8 %fusion = f32[8,128,768]{2,1,0:T(8,128)} fusion(pred[768,768]{1,0:T(8,128)(4,1)S(1)} %iota_compare_fusion, bf16[768,8,128]{0,2,1:T(8,128)(2,1)} %bitcast.59, bf16[96,8,8,128]{3,2,1,0:T(8,128)(2,1)} %fusion.12, bf16[96,8,8,128]{3,2,1,0:T(8,128)(2,1)} %copy-done.9), kind=kOutput, calls=%fused_computation.5 | convolution fusion | flops 2425356288 | bytes 8454144 | tf_op jit(solution)/shard_map/hts,shd->thd/dot_general | solution.py:85
  38.8 60.7 %all-gather.3.cloned.1.call-done = f32[128,128,128]{2,1,0:T(8,128)} async-done(((f32[8,128,128]{2,1,0:T(8,128)}), f32[128,128,128]{2,1,0:T(8,128)}) %all-gather.3.cloned.1.call-update) | async-done | bytes 8388624 | tf_op jit(solution)/shard_map/all_gather | solution.py:13
  99.5 20.0 %while.14 = (s32[]{:T(128)}, f32[8,128,128]{2,1,0:T(8,128)S(1)}, s32[]{:T(128)}, f32[16,8,128,128]{3,2,1,0:T(8,128)}, s32[]{:T(128)}, /*index=5*/s32[]{:T(128)}) while((s32[]{:T(128)}, f32[8,128,128]{2,1,0:T(8,128)S(1)}, s32[]{:T(128)}, f32[16,8,128,128]{3,2,1,0:T(8,128)}, s32[]{:T(128)}, /*index=5*/s32[]{:T(128)}) %tuple.42), condition=%wide.region_1.2_spmd.clone, body=%wide.region_0.1_spmd.clone.sunk | while | flops 393220 | bytes 1572957 | solution.py:21
  99.5 1.2 add_select_fusion.2
  100.7 1.2 add_select_fusion.2
  102.0 1.2 add_select_fusion.2
  103.2 1.2 add_select_fusion.2
  104.5 1.2 add_select_fusion.2
  105.7 1.2 add_select_fusion.2
  107.0 1.2 add_select_fusion.2
  108.2 1.2 add_select_fusion.2
  109.5 1.2 add_select_fusion.2
  110.7 1.2 add_select_fusion.2
  112.0 1.2 add_select_fusion.2
  113.2 1.2 add_select_fusion.2
  114.5 1.2 add_select_fusion.2
  115.7 1.2 add_select_fusion.2
  117.0 1.2 add_select_fusion.2
  118.2 1.2 add_select_fusion.2
  119.5 3.2 %multiply_convert_fusion = bf16[8,128,768]{2,1,0:T(8,128)(2,1)S(1)} fusion(f32[8,128,768]{2,1,0:T(8,128)} %fusion, f32[768]{0:T(1024)S(1)} %multiply_rsqrt_fusion, bf16[96,8,8,128]{3,2,1,0:T(8,128)(2,1)} %fusion.12, f32[8,128,128]{2,1,0:T(8,128)S(1)} %get-tuple-element.81), kind=kOutput, calls=%fused_computation.10 | convolution fusion | flops 203816960 | bytes 6818816 | tf_op jit(solution)/shard_map/thd,hde->the/dot_general | solution.py:86
  122.7 0.2 copy-done.5
  122.9 3.0 %add_convert_fusion = bf16[768,1024]{1,0:T(8,128)(2,1)} fusion(bf16[768,1024]{1,0:T(8,128)(2,1)S(1)} %copy-done.5, bf16[768,1024]{0,1:T(8,128)(2,1)S(1)} %bitcast.61, bf16[1024,1024]{1,0:T(8,128)(2,1)S(1)} %copy-done.4), kind=kOutput, calls=%fused_computation.9 | convolution fusion | flops 1612972032 | bytes 6815744 | tf_op jit(solution)/shard_map/dot_general | solution.py:93
  126.0 2.3 %gather_fusion = bf16[32,1024]{1,0:T(8,128)(2,1)S(1)} fusion(bf16[768,1024]{1,0:T(8,128)(2,1)} %add_convert_fusion, s32[1024]{0:T(1024)S(1)} %pad_clamp_fusion.1), kind=kCustom, calls=%fused_computation | custom fusion | bytes 131200 | tf_op jit(solution)/shard_map/jit(_take)/gather | solution.py:95
  128.2 1.0 fusion.20
  129.2 3.5 %all-to-all-start = ((bf16[16,8,1024]{2,1,0:T(8,128)(2,1)}), bf16[16,8,1024]{2,1,0:T(8,128)(2,1)S(1)}, u32[]{:S(2)}, u32[]{:S(2)}) async-start(bf16[16,8,1024]{2,1,0:T(8,128)(2,1)} %fusion.20), calls=%async_computation | async-start | bytes 524288 | tf_op jit(solution)/shard_map/all_to_all | solution.py:103
  132.8 0.2 fusion.29
  133.0 0.8 gather_fusion.2
  134.0 8.7 %all-to-all-done = bf16[16,8,1024]{2,1,0:T(8,128)(2,1)S(1)} async-done(((bf16[16,8,1024]{2,1,0:T(8,128)(2,1)}), bf16[16,8,1024]{2,1,0:T(8,128)(2,1)S(1)}, u32[]{:S(2)}, u32[]{:S(2)}) %all-to-all-start) | async-done | bytes 262176 | tf_op jit(solution)/shard_map/all_to_all | solution.py:103
  142.8 2.9 %fusion.22 = bf16[16,8,256]{2,1,0:T(8,128)(2,1)} fusion(bf16[1024,256]{1,0:T(8,128)(2,1)S(1)} %copy-done.2, bf16[1024,1024]{1,0:T(8,128)(2,1)} %param.18, bf16[16,8,1024]{2,1,0:T(8,128)(2,1)S(1)} %all-to-all-done), kind=kOutput, calls=%fused_computation.32 | convolution fusion | flops 335839232 | bytes 2949120 | tf_op jit(solution)/shard_map/dot_general | solution.py:39
  145.6 3.5 %all-to-all-start.1 = ((bf16[16,8,256]{2,1,0:T(8,128)(2,1)}), bf16[16,8,256]{2,1,0:T(8,128)(2,1)S(1)}, u32[]{:S(2)}, u32[]{:S(2)}) async-start(bf16[16,8,256]{2,1,0:T(8,128)(2,1)} %fusion.22), calls=%async_computation.1 | async-start | bytes 131072 | tf_op jit(solution)/shard_map/all_to_all | solution.py:107
  149.2 6.8 %all-to-all-done.1 = bf16[16,8,256]{2,1,0:T(8,128)(2,1)S(1)} async-done(((bf16[16,8,256]{2,1,0:T(8,128)(2,1)}), bf16[16,8,256]{2,1,0:T(8,128)(2,1)S(1)}, u32[]{:S(2)}, u32[]{:S(2)}) %all-to-all-start.1) | async-done | bytes 65568 | tf_op jit(solution)/shard_map/all_to_all | solution.py:107
  156.0 0.7 gather_fusion.1
  156.7 0.8 multiply_reduce_fusion
  (42 shorter events, 1.0 us)
Async XLA Ops:
  7.2 1.6 copy-start
  7.2 92.3 %all-gather.3.cloned.1.call-start = ((), (), s32[]{:S(2)}) async-start(), calls=%async_computation.2 | async-start | bytes 8912896 | tf_op jit(solution)/shard_map/all_gather | solution.py:13
  15.7 5.1 %copy-start.1 = (bf16[768,1024]{0,1:T(8,128)(2,1)S(1)}, bf16[768,1024]{0,1:T(8,128)(2,1)}, u32[]{:S(2)}) copy-start(bf16[768,1024]{0,1:T(8,128)(2,1)} %copy.73) | copy-start | bytes 4718596
  19.7 1.1 copy-start.9
  20.9 1.4 copy-start.3
  20.9 2.4 %copy-start.7 = (s32[32]{0:T(128)S(1)}, s32[32]{0:T(128)}, u32[]{:S(2)}) copy-start(s32[32]{0:T(128)} %param.23) | copy-start | bytes 388
  20.9 2.8 %copy-start.8 = (s32[32]{0:T(128)S(1)}, s32[32]{0:T(128)}, u32[]{:S(2)}) copy-start(s32[32]{0:T(128)} %param.21) | copy-start | bytes 388
  119.5 3.3 %copy-start.4 = (bf16[1024,1024]{1,0:T(8,128)(2,1)S(1)}, bf16[1024,1024]{1,0:T(8,128)(2,1)}, u32[]{:S(2)}) copy-start(bf16[1024,1024]{1,0:T(8,128)(2,1)} %param.17) | copy-start | bytes 6291460
  119.5 3.4 %copy-start.5 = (bf16[768,1024]{1,0:T(8,128)(2,1)S(1)}, bf16[768,1024]{1,0:T(8,128)(2,1)}, u32[]{:S(2)}) copy-start(bf16[768,1024]{1,0:T(8,128)(2,1)} %param.13) | copy-start | bytes 4718596
  122.9 9.9 %copy-start.6 = (bf16[1024,32]{0,1:T(8,128)(2,1)S(1)}, bf16[1024,32]{0,1:T(8,128)(2,1)}, u32[]{:S(2)}) copy-start(bf16[1024,32]{0,1:T(8,128)(2,1)} %param.20) | copy-start | bytes 196612
  129.2 13.5 %all-to-all-start = ((bf16[16,8,1024]{2,1,0:T(8,128)(2,1)}), bf16[16,8,1024]{2,1,0:T(8,128)(2,1)S(1)}, u32[]{:S(2)}, u32[]{:S(2)}) async-start(bf16[16,8,1024]{2,1,0:T(8,128)(2,1)} %fusion.20), calls=%async_computation | async-start | bytes 524288 | tf_op jit(solution)/shard_map/all_to_all | solution.py:103
  133.0 9.7 %copy-start.2 = (bf16[1024,256]{1,0:T(8,128)(2,1)S(1)}, bf16[1024,256]{1,0:T(8,128)(2,1)}, u32[]{:S(2)}) copy-start(bf16[1024,256]{1,0:T(8,128)(2,1)} %param.19) | copy-start | bytes 1572868
  145.6 10.4 %all-to-all-start.1 = ((bf16[16,8,256]{2,1,0:T(8,128)(2,1)}), bf16[16,8,256]{2,1,0:T(8,128)(2,1)S(1)}, u32[]{:S(2)}, u32[]{:S(2)}) async-start(bf16[16,8,256]{2,1,0:T(8,128)(2,1)} %fusion.22), calls=%async_computation.1 | async-start | bytes 131072 | tf_op jit(solution)/shard_map/all_to_all | solution.py:107
Sparse Core Ops, SparseCore 0:
  22.4 77.0 all-gather.2
where the time goes:
time: 166 us; the launch traced here: 164 us
  waiting for transfers between devices  76.2 us (46%)
  matrix products  34.8 us (21%)
  other arithmetic  21.1 us (13%)
  between operations  14.3 us (9%)
  local copies, waits for them, and re-layouts  10.5 us (6%)
  starting transfers between devices  7.05 us (4%)
    all_gather x1, waiting for transfers between devices, carried_in(): everything = lax.all_gather(shard, axis)  60.7 us
    select_n x16, other arithmetic, step(): return jnp.where(reached, new, before)  19.6 us
    dot_general x1, matrix products, shards(): jnp.einsum('hts,shd->thd', weight, values, preferred_element_type=jnp.flo...  9.81 us
    all_to_all x1, waiting for transfers between devices, shards(): lax.all_to_all(outgoing, 'seq', split_axis=0, concat_axis=0, tiled=True)  8.73 us
    all_to_all x1, waiting for transfers between devices, shards(): lax.all_to_all(partials.astype(jnp.bfloat16), 'seq', split_axis=0, concat...  6.75 us
    dot_general x1, matrix products, shards(): jnp.dot(events, w_query, preferred_element_type=jnp.float32)  5.01 us
    dot_general x1, matrix products, shards(): jnp.dot(events, w_key, preferred_element_type=jnp.float32)  4.34 us
    dot_general x1, matrix products, shards(): jnp.dot(events, w_value, preferred_element_type=jnp.float32)  3.97 us
  transfers between devices with their start and end apart: 3, of which 3 were waited for; matrix products, arithmetic and copies ran while one was open for 11% of the time, Pallas kernels for 0%

commit v1 on v0

v1 whole, which is shorter than its diff:
```python
import functools

import jax
import jax.numpy as jnp
from jax import lax
from jax.experimental import pallas as pl
from jax.experimental.pallas import tpu as pltpu
from jax.sharding import PartitionSpec as P

HEADS = 8
EXPERTS = 16
CAP = 8
TILE = 256
MESH = pl.DeviceIdType.MESH
F32 = jnp.float32
BF16 = jnp.bfloat16


def dot(a, b):
    return jnp.dot(a, b, preferred_element_type=F32)


def dot_t(a, b):
    return lax.dot_general(a, b, (((1,), (1,)), ((), ())), preferred_element_type=F32)


def t_dot(a, b):
    return lax.dot_general(a, b, (((0,), (0,)), ((), ())), preferred_element_type=F32)


def loop(count, body):
    def step(i, carry):
        body(i)
        return carry

    lax.fori_loop(0, count, step, 0)


def kernel(
    n,
    lab_ref,
    gate_ref,
    ev_hbm,
    wq_hbm,
    wk_hbm,
    wv_hbm,
    wo_hbm,
    win_hbm,
    wout_hbm,
    hid_hbm,
    scores_ref,
    ev,
    wq,
    wk,
    wv,
    wo,
    win,
    wout,
    q_s,
    k_s,
    v_s,
    cum_s,
    within_s,
    att_s,
    hid_s,
    send1,
    recv1,
    pre2,
    pre_r,
    qp_s,
    wp_s,
    attp_s,
    pk_s,
    disp_s,
    arr_r,
    inner_s,
    back_s,
    back_r,
    load_sem,
    kv_sem,
    q_sem,
    o_sem,
    out_sem,
    ss1,
    rs1,
    ss2,
    rs2,
    ss3,
    rs3,
    ss4,
    rs4,
):
    me = lax.axis_index("seq")
    tok, width = ev.shape
    head = width // HEADS
    tiles = width // TILE
    blocks = tok // TILE
    labels = lab_ref.shape[0]
    copies = n // EXPERTS
    part = width // n
    per_head = head // part
    per_tile = n // tiles
    own = lax.rem(me, tiles) * per_tile + me // tiles
    slots = EXPERTS * CAP

    def cols_of(c):
        return pl.ds(pl.multiple_of(c * TILE, TILE), TILE)

    def head_of(h):
        return pl.ds(pl.multiple_of(h * head, head), head)

    def tile_copy(src, dst, sem, c):
        return pltpu.make_async_copy(src.at[:, cols_of(c)], dst.at[:, cols_of(c)], sem)

    def remote(src, dst, send, recv, where):
        return pltpu.make_async_remote_copy(
            src_ref=src,
            dst_ref=dst,
            send_sem=send,
            recv_sem=recv,
            device_id={"seq": where},
            device_id_type=MESH,
        )

    barrier = pltpu.get_barrier_semaphore()

    def greet(o):
        peer = lax.rem(me + o + 1, n)
        pl.semaphore_signal(barrier, inc=1, device_id={"seq": peer}, device_id_type=MESH)

    loop(n - 1, greet)

    ev_copy = pltpu.make_async_copy(ev_hbm, ev, load_sem.at[0])
    ev_copy.start()
    for c in range(tiles):
        tile_copy(wk_hbm, wk, kv_sem.at[0, c], c).start()
        tile_copy(wv_hbm, wv, kv_sem.at[1, c], c).start()
    for c in range(tiles):
        tile_copy(wq_hbm, wq, q_sem.at[c], c).start()
    wo_copy = pltpu.make_async_copy(wo_hbm, wo, load_sem.at[1])
    win_copy = pltpu.make_async_copy(win_hbm, win, load_sem.at[2])
    wout_copy = pltpu.make_async_copy(wout_hbm, wout, load_sem.at[3])
    wo_copy.start()
    win_copy.start()
    wout_copy.start()
    ev_copy.wait()

    def keys_values(c):
        cols = cols_of(c)
        tile_copy(wk_hbm, wk, kv_sem.at[0, c], c).wait()
        k_s[:, cols] = dot(ev[...], wk[:, cols]).astype(BF16)
        tile_copy(wv_hbm, wv, kv_sem.at[1, c], c).wait()
        v_s[:, cols] = dot(ev[...], wv[:, cols]).astype(BF16)
        for hh in range(TILE // head):
            h = c * (TILE // head) + hh
            hc = head_of(h)
            total = None
            for i in range(blocks):
                rows = pl.ds(i * TILE, TILE)
                state = t_dot(k_s[rows, hc], v_s[rows, hc])
                total = state if total is None else total + state
                if i < blocks - 1:
                    cum_s[i, hc, :] = total
            sent = total.astype(BF16)
            for u in range(per_head):
                send1[h * per_head + u] = sent[u * part : (u + 1) * part]

        @pl.when(c == 0)
        def _():
            pl.semaphore_wait(barrier, n - 1)

        def send(u):
            owner = u * tiles + c

            @pl.when(owner != me)
            def _():
                remote(
                    send1.at[c * per_tile + u],
                    recv1.at[me],
                    ss1.at[owner],
                    rs1.at[me],
                    owner,
                ).start()

        loop(per_tile, send)

    loop(tiles, keys_values)

    def queries(c):
        cols = cols_of(c)
        tile_copy(wq_hbm, wq, q_sem.at[c], c).wait()
        q_s[:, cols] = dot(ev[...], wq[:, cols]).astype(BF16)

    loop(tiles, queries)

    recv1[me] = send1[own]

    def await1(s):
        @pl.when(s != me)
        def _():
            remote(send1.at[0], recv1.at[s], ss1.at[s], rs1.at[s], s).wait_recv()

    loop(n, await1)

    def scan(s, acc):
        pre2[s] = acc.astype(BF16)
        return acc + recv1[s].astype(F32)

    lax.fori_loop(0, n, scan, jnp.zeros((part, recv1.shape[2]), F32))
    pre_r[own] = pre2[me]

    def send2(o):
        peer = lax.rem(me + o + 1, n)
        remote(pre2.at[peer], pre_r.at[own], ss2.at[peer], rs2.at[me], peer).start()

    loop(n - 1, send2)

    tri = lax.broadcasted_iota(jnp.int32, (TILE, TILE), 1) <= lax.broadcasted_iota(
        jnp.int32, (TILE, TILE), 0
    )

    def within(h):
        hc = head_of(h)
        for i in range(blocks):
            rows = pl.ds(i * TILE, TILE)
            w = jnp.where(tri, dot_t(q_s[rows, hc], k_s[rows, hc]), 0.0).astype(BF16)
            within_s[rows, hc] = dot(w, v_s[rows, hc])

    loop(HEADS, within)

    lab = lab_ref[...]
    row = lab[:, 0:1]
    first, second, task = lab[:, 1:2], lab[:, 2:3], lab[:, 3:4]
    places = lax.broadcasted_iota(jnp.int32, (labels, tok), 1)
    pick = jnp.where(places == row, 1.0, 0.0).astype(BF16)
    seen = places <= row
    qp_s[...] = dot(pick, q_s[...]).astype(BF16)

    def within_picked(h):
        hc = head_of(h)
        w = jnp.where(seen, dot_t(qp_s[:, hc], k_s[:, hc]), 0.0).astype(BF16)
        wp_s[:, hc] = dot(w, v_s[:, hc])

    loop(HEADS, within_picked)
    slot = lax.broadcasted_iota(jnp.int32, (labels, slots), 1)
    slot_expert, slot_rank = slot // CAP, slot % CAP
    hit0, hit1 = slot_expert == first, slot_expert == second
    named = jnp.where(hit0 | hit1, 1.0, 0.0).astype(BF16)
    lower = jnp.where(
        lax.broadcasted_iota(jnp.int32, (labels, labels), 1)
        < lax.broadcasted_iota(jnp.int32, (labels, labels), 0),
        1.0,
        0.0,
    ).astype(BF16)
    rank = dot(lower, named)
    at_rank = rank == slot_rank.astype(F32)
    sel0, sel1 = hit0 & at_rank, hit1 & at_rank
    selector = jnp.where(sel0 | sel1, 1.0, 0.0).astype(BF16)
    scale_p = lax.rsqrt((me * tok + row + 1).astype(F32) * head)

    def await2(s):
        @pl.when(s != me)
        def _():
            spot = lax.rem(s, tiles) * per_tile + s // tiles
            remote(pre2.at[s], pre_r.at[spot], ss2.at[s], rs2.at[s], s).wait_recv()

    loop(n, await2)

    def prefix_of(h):
        spots = pl.ds(h * per_head, per_head)
        return pre_r[spots].reshape(head, head)

    def attended_picked(h):
        hc = head_of(h)
        earlier = dot(qp_s[:, hc], prefix_of(h))
        attp_s[:, hc] = ((wp_s[:, hc] + earlier) * scale_p).astype(BF16)

    loop(HEADS, attended_picked)
    wo_copy.wait()

    def hidden_picked(c):
        cols = cols_of(c)
        base = dot(pick, ev[:, cols])
        pk_s[:, cols] = (base + dot(attp_s[...], wo[:, cols])).astype(BF16)
        moved = t_dot(selector, pk_s[:, cols])
        disp_s[:, :, cols] = moved.reshape(EXPERTS, CAP, TILE).astype(BF16)

    loop(tiles, hidden_picked)
    arr_r[me] = disp_s[me // copies]

    def send3(o):
        peer = lax.rem(me + o + 1, n)
        remote(
            disp_s.at[peer // copies], arr_r.at[me], ss3.at[peer], rs3.at[me], peer
        ).start()

    loop(n - 1, send3)
    logits = dot(pk_s[...], gate_ref[...])
    column = lax.broadcasted_iota(jnp.int32, logits.shape, 1)

    def gate_of(expert):
        chosen = jnp.where(column == task * EXPERTS + expert, logits, 0.0)
        return jax.nn.sigmoid(jnp.sum(chosen, axis=1, keepdims=True))

    mix = jnp.where(sel0, gate_of(first), 0.0) + jnp.where(sel1, gate_of(second), 0.0)

    def attended(h):
        hc = head_of(h)
        before = prefix_of(h)
        for i in range(blocks):
            rows = pl.ds(i * TILE, TILE)
            state = before if i == 0 else (before.astype(F32) + cum_s[i - 1, hc, :]).astype(BF16)
            place = me * tok + i * TILE + lax.broadcasted_iota(jnp.int32, (TILE, head), 0)
            scale = lax.rsqrt((place + 1).astype(F32) * head)
            att_s[rows, hc] = (
                (within_s[rows, hc] + dot(q_s[rows, hc], state)) * scale
            ).astype(BF16)

    loop(HEADS, attended)

    def hidden(c):
        cols = cols_of(c)
        hid_s[:, cols] = (ev[:, cols].astype(F32) + dot(att_s[...], wo[:, cols])).astype(BF16)
        tile_copy(hid_s, hid_hbm, out_sem.at[c], c).start()

    half = tiles // 2
    loop(half, hidden)

    win_copy.wait()
    wout_copy.wait()

    def await3(s):
        @pl.when(s != me)
        def _():
            remote(disp_s.at[0], arr_r.at[s], ss3.at[s], rs3.at[s], s).wait_recv()

    loop(n, await3)
    units = win.shape[1]
    for c in range(units // TILE):
        cols = pl.ds(c * TILE, TILE)
        arrived = arr_r[...].astype(F32).reshape(n * CAP, width).astype(BF16)
        inner_s[:, cols] = jnp.maximum(dot(arrived, win[:, cols]), 0.0).astype(BF16)
    partial = dot(inner_s[...], wout[...])
    back_s[...] = partial.reshape(n, CAP, partial.shape[1]).astype(BF16)
    back_r[me] = back_s[me]

    def send4(o):
        peer = lax.rem(me + o + 1, n)
        remote(back_s.at[peer], back_r.at[me], ss4.at[peer], rs4.at[me], peer).start()

    loop(n - 1, send4)
    loop(tiles - half, lambda c: hidden(c + half))

    def await4(s):
        @pl.when(s != me)
        def _():
            remote(back_s.at[s], back_r.at[s], ss4.at[s], rs4.at[s], s).wait_recv()

    loop(n, await4)
    back = back_r[...].astype(F32)
    if copies > 1:
        back = back.reshape(EXPERTS, copies, CAP, back.shape[2]).sum(axis=1)
    totals = back.reshape(slots, back.shape[-1])
    scores_ref[...] = jnp.dot(
        mix, totals, preferred_element_type=F32, precision=lax.Precision.HIGHEST
    )

    def sent(s):
        @pl.when(s != me)
        def _():
            remote(send1.at[0], recv1.at[s], ss1.at[s], rs1.at[s], s).wait_send()
            remote(pre2.at[s], pre_r.at[s], ss2.at[s], rs2.at[s], s).wait_send()
            remote(disp_s.at[0], arr_r.at[s], ss3.at[s], rs3.at[s], s).wait_send()
            remote(back_s.at[s], back_r.at[s], ss4.at[s], rs4.at[s], s).wait_send()

    loop(n, sent)
    for c in range(tiles):
        tile_copy(hid_s, hid_hbm, out_sem.at[c], c).wait()


def shards(
    n,
    events,
    w_query,
    w_key,
    w_value,
    w_output,
    expert_in,
    expert_out,
    gate_weight,
    label_rows,
    label_experts,
    label_tasks,
):
    tok, width = events.shape
    head = width // HEADS
    labels = label_rows.shape[0]
    units, out = expert_out.shape
    part = width // n
    tiles = width // TILE
    lab = jnp.concatenate([label_rows[:, None], label_experts, label_tasks[:, None]], axis=1)
    vmem = pl.BlockSpec(memory_space=pltpu.VMEM)
    hbm = pl.BlockSpec(memory_space=pl.ANY)
    dma = pltpu.SemaphoreType.DMA
    return pl.pallas_call(
        functools.partial(kernel, n),
        out_shape=(
            jax.ShapeDtypeStruct((tok, width), BF16),
            jax.ShapeDtypeStruct((labels, out), F32),
        ),
        in_specs=[vmem, vmem] + [hbm] * 7,
        out_specs=(hbm, vmem),
        scratch_shapes=[
            pltpu.VMEM((tok, width), BF16),
            pltpu.VMEM((width, width), BF16),
            pltpu.VMEM((width, width), BF16),
            pltpu.VMEM((width, width), BF16),
            pltpu.VMEM((width, width), BF16),
            pltpu.VMEM((width, units), BF16),
            pltpu.VMEM((units, out), BF16),
            pltpu.VMEM((tok, width), BF16),
            pltpu.VMEM((tok, width), BF16),
            pltpu.VMEM((tok, width), BF16),
            pltpu.VMEM((max(tok // TILE - 1, 1), width, head), F32),
            pltpu.VMEM((tok, width), F32),
            pltpu.VMEM((tok, width), BF16),
            pltpu.VMEM((tok, width), BF16),
            pltpu.VMEM((n, part, head), BF16),
            pltpu.VMEM((n, part, head), BF16),
            pltpu.VMEM((n, part, head), BF16),
            pltpu.VMEM((n, part, head), BF16),
            pltpu.VMEM((labels, width), BF16),
            pltpu.VMEM((labels, width), F32),
            pltpu.VMEM((labels, width), BF16),
            pltpu.VMEM((labels, width), BF16),
            pltpu.VMEM((EXPERTS, CAP, width), BF16),
            pltpu.VMEM((n, CAP, width), BF16),
            pltpu.VMEM((n * CAP, units), BF16),
            pltpu.VMEM((n, CAP, out), BF16),
            pltpu.VMEM((n, CAP, out), BF16),
            dma((4,)),
            dma((2, tiles)),
            dma((tiles,)),
            dma((1,)),
            dma((tiles,)),
        ]
        + [dma((n,))] * 8,
        compiler_params=pltpu.CompilerParams(
            collective_id=0, has_side_effects=True, vmem_limit_bytes=60 << 20
        ),
    )(
        lab,
        gate_weight,
        events,
        w_query,
        w_key,
        w_value,
        w_output,
        expert_in,
        expert_out,
    )


def solution(mesh):
    placed = (
        P(("grp", "seq"), None),
        P(),
        P(),
        P(),
        P(),
        P(None, "seq"),
        P("seq", None),
        P(),
        P(("grp", "seq")),
        P(("grp", "seq"), None),
        P(("grp", "seq")),
    )
    return jax.shard_map(
        functools.partial(shards, mesh.shape["seq"]),
        mesh=mesh,
        in_specs=placed,
        out_specs=(P(("grp", "seq"), None), P(("grp", "seq"), None)),
        check_vma=False,
    )
```

time: 166 us -> 51.4 us (0.31)
  waiting for transfers between devices: 76.2 us -> 0 us
  Pallas kernels: 0 us -> 44.1 us
  matrix products: 34.8 us -> 0 us
  other arithmetic: 21.1 us -> 0.7 us
  between operations: 14.3 us -> 0.65 us
  starting transfers between devices: 7.05 us -> 0 us
  local copies, waits for them, and re-layouts: 10.5 us -> 5.67 us
    all_gather x1 -> x0, waiting for transfers between devices: 60.7 us -> none  [carried_in(): everything = lax.all_gather(shard, axis)]
    pallas_call x0 -> x1, Pallas kernels: none -> 44.1 us  [shards(): pl.pallas_call(functools.partial(kernel, n), out_shape=(jax.ShapeDtypeStr...]
    dot_general x10 -> x0, matrix products: 34.8 us -> none  [the longest x1 9.81 us: shards(): jnp.einsum('hts,shd->thd', weight, values, preferred_element_type=jnp.flo...]
    select_n x18 -> x0, other arithmetic: 19.6 us -> none  [the longest x16 19.6 us: step(): return jnp.where(reached, new, before)]
    all_to_all x2 -> x0, waiting for transfers between devices: 15.5 us -> none  [the longest x1 8.73 us: shards(): lax.all_to_all(outgoing, 'seq', split_axis=0, concat_axis=0, tiled=True)]
    all_to_all x2 -> x0, starting transfers between devices: 7.01 us -> none  [the longest x1 3.53 us: shards(): lax.all_to_all(outgoing, 'seq', split_axis=0, concat_axis=0, tiled=True)]
    gather x8 -> x0, local copies, waits for them, and re-layouts: 4.17 us -> none  [the longest x1 2.28 us: shards(): picked = jnp.take(hidden, label_rows, axis=0)]
    reshape x2 -> x0, local copies, waits for them, and re-layouts: 2.72 us -> none  [the longest x1 2.62 us: shards(): keys = jnp.dot(events, w_key, preferred_element_type=jnp.float32).astype(...]
  transfers between devices with their start and end apart: 3 -> 0, of which waited for: 3 -> 0; matrix products, arithmetic and copies ran while one was open for 11% -> 0% of each run, Pallas kernels for 0% -> 0%
where the time goes in v1:
time: 51.4 us; the launch traced here: 51.1 us
  Pallas kernels  44.1 us (86%)
  local copies, waits for them, and re-layouts  5.67 us (11%)
  other arithmetic  0.7 us (1%)
  between operations  0.65 us (1%)
    pallas_call x1, Pallas kernels, shards(): pl.pallas_call(functools.partial(kernel, n), out_shape=(jax.ShapeDtypeStr...  44.1 us
    unnamed x5, local copies, waits for them, and re-layouts  4.97 us

profile of v1, /device:TPU:0, one launch (start us, length us, event | category | flops | bytes accessed | tf_op | source)
XLA Modules:
  0.0 51.1 jit_solution(14258880462688218608)
XLA Ops:
  0.6 0.7 %pad_add_fusion = s32[32,4]{0,1:T(4,128)S(1)} fusion(s32[32,1]{0,1:T(1,128)} %bitcast.2, s32[32,2]{0,1:T(2,128)} %param.20, s32[32,1]{0,1:T(1,128)} %bitcast.3), kind=kLoop, calls=%fused_computation | loop fusion | flops 256 | bytes 1024 | tf_op jit(solution)/shard_map/concatenate | solution.py:401
  1.3 0.7 %copy.17.lab_ref = s32[32,4]{1,0:T(8,128)} copy(s32[32,4]{0,1:T(4,128)S(1)} %pad_add_fusion) | data formatting | bytes 1024 | tf_op jit(solution)/shard_map/concatenate | solution.py:401
  2.0 1.7 %copy.18.gate_ref = bf16[1024,32]{1,0:T(8,128)(2,1)} copy(bf16[1024,32]{0,1:T(8,128)(2,1)} %param.18) | data formatting | bytes 131072 | tf_op args[7]
  3.7 44.1 %shard_map.122 = (bf16[768,1024]{1,0:T(8,128)(2,1)}, f32[32,256]{1,0:T(8,128)}) custom-call(s32[32,4]{1,0:T(8,128)} %copy.17.lab_ref, bf16[1024,32]{1,0:T(8,128)(2,1)} %copy.18.gate_ref, bf16[768,1024]{1,0:T(8,128)(2,1)} %ev_hbm.1, bf16[1024,1024]{1,0:T(8,128)(2,1)} %wq_hbm.1, bf16[1024,1024]{1,0:T(8,128)(2,1)} %wk_hbm.1, bf16[1024,1024]{1,0:T(8,128)(2,1)} %wv_hbm.1, ...), custom_call_target="tpu_custom_call" | custom-call | tf_op jit(solution)/shard_map/pallas_call | solution.py:405
  47.8 0.0 copy-start
  47.8 2.7 %copy.21 = bf16[768,1024]{1,0:T(8,128)(2,1)} copy(bf16[768,1024]{1,0:T(8,128)(2,1)} %get-tuple-element.4) | data formatting | bytes 3145728
  50.5 0.0 copy-done
  50.5 0.6 %copy.22 = f32[32,256]{1,0:T(8,128)} copy(f32[32,256]{1,0:T(8,128)S(1)} %copy-done) | data formatting | bytes 65536
Async XLA Ops:
  47.8 2.7 %copy-start = (f32[32,256]{1,0:T(8,128)S(1)}, f32[32,256]{1,0:T(8,128)}, u32[]{:S(2)}) copy-start(f32[32,256]{1,0:T(8,128)} %get-tuple-element.5) | copy-start | bytes 98308

commit v2 on v1

--- a/solution.py
+++ b/solution.py
@@ -38,8 +38,10 @@
 
 def kernel(
     n,
-    lab_ref,
-    gate_ref,
+    rows_hbm,
+    experts_hbm,
+    tasks_hbm,
+    gate_hbm,
     ev_hbm,
     wq_hbm,
     wk_hbm,
@@ -47,8 +49,12 @@
     wo_hbm,
     win_hbm,
     wout_hbm,
-    hid_hbm,
+    hid_s,
     scores_ref,
+    rows_s,
+    experts_s,
+    tasks_s,
+    gate_s,
     ev,
     wq,
     wk,
@@ -62,13 +68,13 @@
     cum_s,
     within_s,
     att_s,
-    hid_s,
     send1,
     recv1,
     pre2,
     pre_r,
     qp_s,
     wp_s,
+    evp_s,
     attp_s,
     pk_s,
     disp_s,
@@ -79,8 +85,7 @@
     load_sem,
     kv_sem,
     q_sem,
-    o_sem,
-    out_sem,
+    small_sem,
     ss1,
     rs1,
     ss2,
@@ -95,7 +100,7 @@
     head = width // HEADS
     tiles = width // TILE
     blocks = tok // TILE
-    labels = lab_ref.shape[0]
+    labels = rows_s.shape[1]
     copies = n // EXPERTS
     part = width // n
     per_head = head // part
@@ -140,6 +145,19 @@
     wo_copy = pltpu.make_async_copy(wo_hbm, wo, load_sem.at[1])
     win_copy = pltpu.make_async_copy(win_hbm, win, load_sem.at[2])
     wout_copy = pltpu.make_async_copy(wout_hbm, wout, load_sem.at[3])
+    small = [
+        pltpu.make_async_copy(src, dst, small_sem.at[i])
+        for i, (src, dst) in enumerate(
+            (
+                (rows_hbm, rows_s),
+                (experts_hbm, experts_s),
+                (tasks_hbm, tasks_s),
+                (gate_hbm, gate_s),
+            )
+        )
+    ]
+    for copy in small:
+        copy.start()
     wo_copy.start()
     win_copy.start()
     wout_copy.start()
@@ -210,10 +228,13 @@
     pre_r[own] = pre2[me]
 
     def send2(o):
-        peer = lax.rem(me + o + 1, n)
-        remote(pre2.at[peer], pre_r.at[own], ss2.at[peer], rs2.at[me], peer).start()
-
-    loop(n - 1, send2)
+        peer = lax.rem(me + n // 2 + o, n)
+
+        @pl.when(peer != me)
+        def _():
+            remote(pre2.at[peer], pre_r.at[own], ss2.at[peer], rs2.at[me], peer).start()
+
+    loop(n, send2)
 
     tri = lax.broadcasted_iota(jnp.int32, (TILE, TILE), 1) <= lax.broadcasted_iota(
         jnp.int32, (TILE, TILE), 0
@@ -228,9 +249,18 @@
 
     loop(HEADS, within)
 
-    lab = lab_ref[...]
-    row = lab[:, 0:1]
-    first, second, task = lab[:, 1:2], lab[:, 2:3], lab[:, 3:4]
+    for copy in small:
+        copy.wait()
+    diagonal = lax.broadcasted_iota(jnp.int32, (labels, labels), 0) == lax.broadcasted_iota(
+        jnp.int32, (labels, labels), 1
+    )
+
+    def column_of(line):
+        return jnp.sum(jnp.where(diagonal, line, 0), axis=1, keepdims=True)
+
+    row = column_of(rows_s[...])
+    first, second = column_of(experts_s[0:1, :]), column_of(experts_s[1:2, :])
+    task = column_of(tasks_s[...])
     places = lax.broadcasted_iota(jnp.int32, (labels, tok), 1)
     pick = jnp.where(places == row, 1.0, 0.0).astype(BF16)
     seen = places <= row
@@ -242,6 +272,12 @@
         wp_s[:, hc] = dot(w, v_s[:, hc])
 
     loop(HEADS, within_picked)
+
+    def events_picked(c):
+        cols = cols_of(c)
+        evp_s[:, cols] = dot(pick, ev[:, cols])
+
+    loop(tiles, events_picked)
     slot = lax.broadcasted_iota(jnp.int32, (labels, slots), 1)
     slot_expert, slot_rank = slot // CAP, slot % CAP
     hit0, hit1 = slot_expert == first, slot_expert == second
@@ -280,8 +316,7 @@
 
     def hidden_picked(c):
         cols = cols_of(c)
-        base = dot(pick, ev[:, cols])
-        pk_s[:, cols] = (base + dot(attp_s[...], wo[:, cols])).astype(BF16)
+        pk_s[:, cols] = (evp_s[:, cols] + dot(attp_s[...], wo[:, cols])).astype(BF16)
         moved = t_dot(selector, pk_s[:, cols])
         disp_s[:, :, cols] = moved.reshape(EXPERTS, CAP, TILE).astype(BF16)
 
@@ -289,13 +324,16 @@
     arr_r[me] = disp_s[me // copies]
 
     def send3(o):
-        peer = lax.rem(me + o + 1, n)
-        remote(
-            disp_s.at[peer // copies], arr_r.at[me], ss3.at[peer], rs3.at[me], peer
-        ).start()
-
-    loop(n - 1, send3)
-    logits = dot(pk_s[...], gate_ref[...])
+        peer = lax.rem(me + n // 2 + o, n)
+
+        @pl.when(peer != me)
+        def _():
+            remote(
+                disp_s.at[peer // copies], arr_r.at[me], ss3.at[peer], rs3.at[me], peer
+            ).start()
+
+    loop(n, send3)
+    logits = dot_t(pk_s[...], gate_s[...])
     column = lax.broadcasted_iota(jnp.int32, logits.shape, 1)
 
     def gate_of(expert):
@@ -321,7 +359,6 @@
     def hidden(c):
         cols = cols_of(c)
         hid_s[:, cols] = (ev[:, cols].astype(F32) + dot(att_s[...], wo[:, cols])).astype(BF16)
-        tile_copy(hid_s, hid_hbm, out_sem.at[c], c).start()
 
     half = tiles // 2
     loop(half, hidden)
@@ -345,10 +382,13 @@
     back_r[me] = back_s[me]
 
     def send4(o):
-        peer = lax.rem(me + o + 1, n)
-        remote(back_s.at[peer], back_r.at[me], ss4.at[peer], rs4.at[me], peer).start()
-
-    loop(n - 1, send4)
+        peer = lax.rem(me + n // 2 + o, n)
+
+        @pl.when(peer != me)
+        def _():
+            remote(back_s.at[peer], back_r.at[me], ss4.at[peer], rs4.at[me], peer).start()
+
+    loop(n, send4)
     loop(tiles - half, lambda c: hidden(c + half))
 
     def await4(s):
@@ -374,8 +414,6 @@
             remote(back_s.at[s], back_r.at[s], ss4.at[s], rs4.at[s], s).wait_send()
 
     loop(n, sent)
-    for c in range(tiles):
-        tile_copy(hid_s, hid_hbm, out_sem.at[c], c).wait()
 
 
 def shards(
@@ -398,9 +436,8 @@
     units, out = expert_out.shape
     part = width // n
     tiles = width // TILE
-    lab = jnp.concatenate([label_rows[:, None], label_experts, label_tasks[:, None]], axis=1)
     vmem = pl.BlockSpec(memory_space=pltpu.VMEM)
-    hbm = pl.BlockSpec(memory_space=pl.ANY)
+    hbm = pl.BlockSpec(memory_space=pltpu.HBM)
     dma = pltpu.SemaphoreType.DMA
     return pl.pallas_call(
         functools.partial(kernel, n),
@@ -408,9 +445,13 @@
             jax.ShapeDtypeStruct((tok, width), BF16),
             jax.ShapeDtypeStruct((labels, out), F32),
         ),
-        in_specs=[vmem, vmem] + [hbm] * 7,
-        out_specs=(hbm, vmem),
+        in_specs=[hbm] * 11,
+        out_specs=(vmem, vmem),
         scratch_shapes=[
+            pltpu.VMEM((1, labels), jnp.int32),
+            pltpu.VMEM((2, labels), jnp.int32),
+            pltpu.VMEM((1, labels), jnp.int32),
+            pltpu.VMEM((gate_weight.shape[1], width), BF16),
             pltpu.VMEM((tok, width), BF16),
             pltpu.VMEM((width, width), BF16),
             pltpu.VMEM((width, width), BF16),
@@ -424,12 +465,12 @@
             pltpu.VMEM((max(tok // TILE - 1, 1), width, head), F32),
             pltpu.VMEM((tok, width), F32),
             pltpu.VMEM((tok, width), BF16),
-            pltpu.VMEM((tok, width), BF16),
             pltpu.VMEM((n, part, head), BF16),
             pltpu.VMEM((n, part, head), BF16),
             pltpu.VMEM((n, part, head), BF16),
             pltpu.VMEM((n, part, head), BF16),
             pltpu.VMEM((labels, width), BF16),
+            pltpu.VMEM((labels, width), F32),
             pltpu.VMEM((labels, width), F32),
             pltpu.VMEM((labels, width), BF16),
             pltpu.VMEM((labels, width), BF16),
@@ -441,23 +482,29 @@
             dma((4,)),
             dma((2, tiles)),
             dma((tiles,)),
-            dma((1,)),
-            dma((tiles,)),
+            dma((4,)),
         ]
         + [dma((n,))] * 8,
         compiler_params=pltpu.CompilerParams(
-            collective_id=0, has_side_effects=True, vmem_limit_bytes=60 << 20
+            collective_id=0, has_side_effects=True, vmem_limit_bytes=40 << 20
         ),
     )(
-        lab,
-        gate_weight,
-        events,
-        w_query,
-        w_key,
-        w_value,
-        w_output,
-        expert_in,
-        expert_out,
+        *[
+            pltpu.with_memory_space_constraint(x, pltpu.HBM)
+            for x in (
+                label_rows.reshape(1, labels),
+                label_experts.T,
+                label_tasks.reshape(1, labels),
+                gate_weight.T,
+                events,
+                w_query,
+                w_key,
+                w_value,
+                w_output,
+                expert_in,
+                expert_out,
+            )
+        ]
     )
 
 

time: 51.4 us -> 46 us (0.89)
  local copies, waits for them, and re-layouts: 5.67 us -> 1.76 us
  Pallas kernels: 44.1 us -> 43.4 us
  other arithmetic: 0.7 us -> 0 us
    unnamed x5 -> x2, local copies, waits for them, and re-layouts: 4.97 us -> 1.76 us
    concatenate x1 -> x0, other arithmetic: 0.7 us -> none  [shards(): jnp.concatenate([label_rows[:, None], label_experts, label_tasks[:, None]...]
    concatenate x1 -> x0, local copies, waits for them, and re-layouts: 0.69 us -> none  [shards(): jnp.concatenate([label_rows[:, None], label_experts, label_tasks[:, None]...]
    pallas_call x1, Pallas kernels: 44.1 us -> 43.4 us  [shards(): pl.pallas_call(functools.partial(kernel, n), out_shape=(jax.ShapeDtypeStr...]
where the time goes in v2:
time: 46 us; the launch traced here: 45.8 us
  Pallas kernels  43.4 us (94%)
  local copies, waits for them, and re-layouts  1.76 us (4%)
  between operations  0.64 us (1%)
    pallas_call x1, Pallas kernels, shards(): pl.pallas_call(functools.partial(kernel, n), out_shape=(jax.ShapeDtypeStr...  43.4 us
    unnamed x2, local copies, waits for them, and re-layouts  1.76 us

profile of v2, /device:TPU:0, one launch (start us, length us, event | category | flops | bytes accessed | tf_op | source)
XLA Modules:
  0.0 45.8 jit_solution(5900470358032751549)
XLA Ops:
  0.6 43.4 %shard_map.122 = (bf16[768,1024]{1,0:T(8,128)(2,1)S(1)}, f32[32,256]{1,0:T(8,128)S(1)}) custom-call(s32[1,32]{1,0:T(1,128)} %bitcast.6, s32[2,32]{1,0:T(2,128)} %bitcast.5, s32[1,32]{1,0:T(1,128)} %bitcast.7, bf16[32,1024]{1,0:T(8,128)(2,1)} %bitcast.4, bf16[768,1024]{1,0:T(8,128)(2,1)} %ev_hbm.1, bf16[1024,1024]{1,0:T(8,128)(2,1)} %wq_hbm.1, ...), custom_call_target="tpu_custom_call" | custom-call | tf_op jit(solution)/shard_map/pallas_call | solution.py:442
  44.1 1.1 %copy.15 = bf16[768,1024]{1,0:T(8,128)(2,1)} copy(bf16[768,1024]{1,0:T(8,128)(2,1)S(1)} %get-tuple-element.4) | data formatting | bytes 3145728
  45.2 0.6 %copy.16 = f32[32,256]{1,0:T(8,128)} copy(f32[32,256]{1,0:T(8,128)S(1)} %get-tuple-element.5) | data formatting | bytes 65536

commit v3 on v2

--- a/solution.py
+++ b/solution.py
@@ -28,12 +28,15 @@
     return lax.dot_general(a, b, (((0,), (0,)), ((), ())), preferred_element_type=F32)
 
 
-def loop(count, body):
+def loop(count, body, wide=1):
+    wide = wide if count % wide == 0 else 1
+
     def step(i, carry):
-        body(i)
+        for j in range(wide):
+            body(i * wide + j)
         return carry
 
-    lax.fori_loop(0, count, step, 0)
+    lax.fori_loop(0, count // wide, step, 0)
 
 
 def kernel(
@@ -228,7 +231,7 @@
     pre_r[own] = pre2[me]
 
     def send2(o):
-        peer = lax.rem(me + n // 2 + o, n)
+        peer = lax.rem(me + o, n)
 
         @pl.when(peer != me)
         def _():
@@ -247,7 +250,7 @@
             w = jnp.where(tri, dot_t(q_s[rows, hc], k_s[rows, hc]), 0.0).astype(BF16)
             within_s[rows, hc] = dot(w, v_s[rows, hc])
 
-    loop(HEADS, within)
+    loop(HEADS, within, 2)
 
     for copy in small:
         copy.wait()
@@ -271,13 +274,13 @@
         w = jnp.where(seen, dot_t(qp_s[:, hc], k_s[:, hc]), 0.0).astype(BF16)
         wp_s[:, hc] = dot(w, v_s[:, hc])
 
-    loop(HEADS, within_picked)
+    loop(HEADS, within_picked, 4)
 
     def events_picked(c):
         cols = cols_of(c)
         evp_s[:, cols] = dot(pick, ev[:, cols])
 
-    loop(tiles, events_picked)
+    loop(tiles, events_picked, 4)
     slot = lax.broadcasted_iota(jnp.int32, (labels, slots), 1)
     slot_expert, slot_rank = slot // CAP, slot % CAP
     hit0, hit1 = slot_expert == first, slot_expert == second
@@ -311,7 +314,7 @@
         earlier = dot(qp_s[:, hc], prefix_of(h))
         attp_s[:, hc] = ((wp_s[:, hc] + earlier) * scale_p).astype(BF16)
 
-    loop(HEADS, attended_picked)
+    loop(HEADS, attended_picked, 8)
     wo_copy.wait()
 
     def hidden_picked(c):
@@ -320,11 +323,11 @@
         moved = t_dot(selector, pk_s[:, cols])
         disp_s[:, :, cols] = moved.reshape(EXPERTS, CAP, TILE).astype(BF16)
 
-    loop(tiles, hidden_picked)
+    loop(tiles, hidden_picked, 4)
     arr_r[me] = disp_s[me // copies]
 
     def send3(o):
-        peer = lax.rem(me + n // 2 + o, n)
+        peer = lax.rem(me + o, n)
 
         @pl.when(peer != me)
         def _():
@@ -354,7 +357,7 @@
                 (within_s[rows, hc] + dot(q_s[rows, hc], state)) * scale
             ).astype(BF16)
 
-    loop(HEADS, attended)
+    loop(HEADS, attended, 2)
 
     def hidden(c):
         cols = cols_of(c)
@@ -382,7 +385,7 @@
     back_r[me] = back_s[me]
 
     def send4(o):
-        peer = lax.rem(me + n // 2 + o, n)
+        peer = lax.rem(me + o, n)
 
         @pl.when(peer != me)
         def _():

time: 46 us -> 43.4 us (0.943)
  Pallas kernels: 43.4 us -> 40.9 us
    pallas_call x1, Pallas kernels: 43.4 us -> 40.9 us  [shards(): pl.pallas_call(functools.partial(kernel, n), out_shape=(jax.ShapeDtypeStr...]
where the time goes in v3:
time: 43.4 us; the launch traced here: 43.3 us
  Pallas kernels  40.9 us (94%)
  local copies, waits for them, and re-layouts  1.76 us (4%)
  between operations  0.64 us (1%)
    pallas_call x1, Pallas kernels, shards(): pl.pallas_call(functools.partial(kernel, n), out_shape=(jax.ShapeDtypeStr...  40.9 us
    unnamed x2, local copies, waits for them, and re-layouts  1.76 us

profile of v3, /device:TPU:0, one launch (start us, length us, event | category | flops | bytes accessed | tf_op | source)
XLA Modules:
  0.0 43.3 jit_solution(2090162912174059420)
XLA Ops:
  0.6 40.9 %shard_map.122 = (bf16[768,1024]{1,0:T(8,128)(2,1)S(1)}, f32[32,256]{1,0:T(8,128)S(1)}) custom-call(s32[1,32]{1,0:T(1,128)} %bitcast.6, s32[2,32]{1,0:T(2,128)} %bitcast.5, s32[1,32]{1,0:T(1,128)} %bitcast.7, bf16[32,1024]{1,0:T(8,128)(2,1)} %bitcast.4, bf16[768,1024]{1,0:T(8,128)(2,1)} %ev_hbm.1, bf16[1024,1024]{1,0:T(8,128)(2,1)} %wq_hbm.1, ...), custom_call_target="tpu_custom_call" | custom-call | tf_op jit(solution)/shard_map/pallas_call | solution.py:445
  41.5 1.1 %copy.15 = bf16[768,1024]{1,0:T(8,128)(2,1)} copy(bf16[768,1024]{1,0:T(8,128)(2,1)S(1)} %get-tuple-element.4) | data formatting | bytes 3145728
  42.7 0.6 %copy.16 = f32[32,256]{1,0:T(8,128)} copy(f32[32,256]{1,0:T(8,128)S(1)} %get-tuple-element.5) | data formatting | bytes 65536

commit v4 on v3

--- a/solution.py
+++ b/solution.py
@@ -231,7 +231,7 @@
     pre_r[own] = pre2[me]
 
     def send2(o):
-        peer = lax.rem(me + o, n)
+        peer = lax.rem(me + n // 2 + o, n)
 
         @pl.when(peer != me)
         def _():
@@ -327,7 +327,7 @@
     arr_r[me] = disp_s[me // copies]
 
     def send3(o):
-        peer = lax.rem(me + o, n)
+        peer = lax.rem(me + n // 2 + o, n)
 
         @pl.when(peer != me)
         def _():
@@ -385,7 +385,7 @@
     back_r[me] = back_s[me]
 
     def send4(o):
-        peer = lax.rem(me + o, n)
+        peer = lax.rem(me + n // 2 + o, n)
 
         @pl.when(peer != me)
         def _():

time: 43.4 us -> 42.6 us (0.982)
  Pallas kernels: 40.9 us -> 40 us
    pallas_call x1, Pallas kernels: 40.9 us -> 40 us  [shards(): pl.pallas_call(functools.partial(kernel, n), out_shape=(jax.ShapeDtypeStr...]
where the time goes in v4:
time: 42.6 us; the launch traced here: 42.4 us
  Pallas kernels  40 us (94%)
  local copies, waits for them, and re-layouts  1.76 us (4%)
  between operations  0.64 us (2%)
    pallas_call x1, Pallas kernels, shards(): pl.pallas_call(functools.partial(kernel, n), out_shape=(jax.ShapeDtypeStr...  40 us
    unnamed x2, local copies, waits for them, and re-layouts  1.76 us

profile of v4, /device:TPU:0, one launch (start us, length us, event | category | flops | bytes accessed | tf_op | source)
XLA Modules:
  0.0 42.4 jit_solution(6831564871491176372)
XLA Ops:
  0.6 40.0 %shard_map.122 = (bf16[768,1024]{1,0:T(8,128)(2,1)S(1)}, f32[32,256]{1,0:T(8,128)S(1)}) custom-call(s32[1,32]{1,0:T(1,128)} %bitcast.6, s32[2,32]{1,0:T(2,128)} %bitcast.5, s32[1,32]{1,0:T(1,128)} %bitcast.7, bf16[32,1024]{1,0:T(8,128)(2,1)} %bitcast.4, bf16[768,1024]{1,0:T(8,128)(2,1)} %ev_hbm.1, bf16[1024,1024]{1,0:T(8,128)(2,1)} %wq_hbm.1, ...), custom_call_target="tpu_custom_call" | custom-call | tf_op jit(solution)/shard_map/pallas_call | solution.py:445
  40.6 1.1 %copy.15 = bf16[768,1024]{1,0:T(8,128)(2,1)} copy(bf16[768,1024]{1,0:T(8,128)(2,1)S(1)} %get-tuple-element.4) | data formatting | bytes 3145728
  41.8 0.6 %copy.16 = f32[32,256]{1,0:T(8,128)} copy(f32[32,256]{1,0:T(8,128)S(1)} %get-tuple-element.5) | data formatting | bytes 65536
